TPU v7x, 256 devices: a whole 4x4x8 slice. The times are simulated.
256 devices in a mesh: seq: 16 (over y, z_lo, core), head: 16 (over z_hi, x).
Axes of the slice: x: 4, y: 4, z: 8 (z_hi: 4, z_lo: 2; z = z_hi * 2 + z_lo), core: 2. Of those that a mesh axis runs over, the one named last changes fastest.
Arguments:
- query_latent: bfloat16 [4096, 128, 576], P('seq', 'head'), may hold values from -6 to 6
- key_latent: bfloat16 [2048, 576], P('seq'), may hold values from -6 to 6
- normalizer: float32 [4096, 128], P('seq', 'head'), may hold values from 7 to 9
- index_query: bfloat16 [4096, 64, 128], P('seq', 'head'), may hold values from -20 to 20
- index_key: bfloat16 [2048, 128], P('seq'), may hold values from -6.5 to 6.5
- index_weight: float32 [4096, 64], P('seq', 'head'), may hold values from 0.05 to 0.5
- kept: int32 [32, 16], P('seq'), may hold values from 0 to 1, as said below
Outputs:
- index_query_grad: bfloat16 [4096, 64, 128], P('seq', 'head')
- index_key_grad: float32 [2048, 128], P('seq')
Inputs may be any that keep to these rules, and one draw needn't show every extreme that they name: `kept`: every query tile keeps the key tile whose position matches its own block of 256 queries.
All inputs are finite; a program needn't handle non-finite values.
Results may differ from a plain program's by a relative error of at most 0.009.
Values may be sent and summed in bfloat16 or wider, within the bound.
No kernel may reach another device: no remote copies, remote signals or barrier semaphores. Data moves between devices by JAX's collectives and lax.ppermute only.
A program may use at most 64 MiB of HBM per device.

v0:
```python
import jax
import jax.numpy as jnp
from jax import lax
from jax.sharding import PartitionSpec as P

attn_scale = 192.0 ** (-0.5)


def joined_along(tiles, dim):
    dims = list(tiles.shape[1:])
    dims[dim] *= tiles.shape[0]
    return jnp.moveaxis(tiles, 0, dim).reshape(dims)


def from_everyone(value, axis):
    copies = jnp.broadcast_to(value, (lax.axis_size(axis), *value.shape))
    return lax.all_to_all(copies, axis, split_axis=0, concat_axis=0, tiled=True)


def gathered_copies(value, axis, dim):
    return joined_along(from_everyone(value, axis), dim)


def sent_together(arrays, axis, dim, along):
    widths = [a.shape[along] for a in arrays]
    both = jnp.concatenate(arrays, axis=along)
    out = lax.psum_scatter(both, axis, scatter_dimension=dim, tiled=True)
    return tuple(jnp.split(out, [sum(widths[:k]) for k in range(1, len(widths))], axis=along))


def cut_along(value, dim, count):
    before, after = (value.shape[:dim], value.shape[dim + 1 :])
    return jnp.moveaxis(value.reshape(*before, count, -1, *after), dim, 0)


def sent_and_summed(value, axis, dim):
    count = lax.axis_size(axis)
    tiles = lax.all_to_all(cut_along(value, dim, count), axis, 0, 0, tiled=True)
    return jnp.sum(tiles.astype(jnp.float32), axis=0)


def of_everyone(value, axis):
    return from_everyone(value, axis).astype(jnp.float32).sum(axis=0)


def logit_gradient(head_sum, logit, keep):
    target = head_sum / jnp.sum(head_sum, axis=1, keepdims=True)
    top = jnp.max(jnp.where(keep, logit, -jnp.inf), axis=1, keepdims=True)
    expo = jnp.where(keep, jnp.exp(jnp.where(keep, logit, top) - top), 0.0)
    return expo / jnp.sum(expo, axis=1, keepdims=True) - target


def local(query_latent, key_latent, normalizer, index_query, index_key, index_weight, kept):
    query_rows, head_count, width = query_latent.shape
    tile_rows = index_key.shape[0]
    index_scale = index_query.shape[2] ** (-0.5)
    keys_whole = gathered_copies(index_key, "seq", 0)
    allow = jnp.repeat(jnp.repeat(kept, tile_rows, axis=0), tile_rows, axis=1) > 0
    z_val = (
        jnp.einsum("tjd,sd->tjs", index_query, keys_whole, preferred_element_type=jnp.float32)
        * index_scale
    )
    logit_part = jnp.sum(index_weight[:, :, None] * jnp.maximum(z_val, 0.0), axis=1)
    flat_query = query_latent.reshape(query_rows * head_count, width)
    piece = lax.all_gather(key_latent, "seq", axis=0, tiled=True)
    count = piece.shape[0]
    scores = (
        jnp.einsum("rc,sc->rs", flat_query, piece, preferred_element_type=jnp.float32) * attn_scale
    )
    prob = jnp.exp(scores.reshape(query_rows, head_count, count) - normalizer[:, :, None])
    partial_value = jnp.where(allow, jnp.sum(prob, axis=1), 0.0)
    head_sum, logit = sent_together((partial_value, logit_part), "head", 0, 1)
    share = head_sum.shape[0]
    begin = lax.axis_index("head") * share
    keep_share = lax.dynamic_slice_in_dim(allow, begin, share, 0)
    gradient = lax.all_gather(
        logit_gradient(head_sum, logit, keep_share), "head", axis=0, tiled=True
    )
    dz_val = jnp.where(z_val > 0, gradient[:, None, :] * index_weight[:, :, None], 0.0).astype(
        jnp.bfloat16
    )
    dquery = (
        jnp.einsum("tjs,sd->tjd", dz_val, keys_whole, preferred_element_type=jnp.float32)
        * index_scale
    ).astype(jnp.bfloat16)
    dkey = sent_and_summed(
        (
            jnp.einsum("tjs,tjd->sd", dz_val, index_query, preferred_element_type=jnp.float32)
            * index_scale
        ).astype(jnp.bfloat16),
        "seq",
        0,
    )
    dkey = of_everyone(dkey.astype(jnp.bfloat16), "head").astype(jnp.float32)
    return (dquery, dkey)


def solution(mesh):
    return jax.shard_map(
        local,
        mesh=mesh,
        in_specs=(
            P("seq", "head", None),
            P("seq", None),
            P("seq", "head"),
            P("seq", "head", None),
            P("seq", None),
            P("seq", "head"),
            P("seq", None),
        ),
        out_specs=(P("seq", "head", None), P("seq", None)),
        check_vma=False,
    )
```

profile of v0, /device:TPU:32, one launch (start us, length us, event | category | flops | bytes accessed | tf_op | source)
XLA Modules:
  0.0 279.0 jit_solution(5726327886860402368)
XLA Ops:
  7.9 1.6 broadcast_in_dim.40
  9.5 5.9 %all-to-all-start = ((bf16[16,128,128]{2,1,0:T(8,128)(2,1)}), bf16[16,128,128]{2,1,0:T(8,128)(2,1)S(1)}, u32[]{:S(2)}, u32[]{:S(2)}) async-start(bf16[16,128,128]{2,1,0:T(8,128)(2,1)} %broadcast_in_dim.40), calls=%async_computation | async-start | bytes 1048576 | tf_op jit(solution)/shard_map/all_to_all | solution.py:17
  15.5 0.8 copy.22
  16.4 4.9 %copy.21 = bf16[256,8,576]{2,1,0:T(8,128)(2,1)} copy(bf16[256,8,576]{0,2,1:T(8,128)(2,1)} %param.7) | data formatting | bytes 4718592 | tf_op args[0]
  22.0 3.2 %all-to-all-done = bf16[16,128,128]{2,1,0:T(8,128)(2,1)S(1)} async-done(((bf16[16,128,128]{2,1,0:T(8,128)(2,1)}), bf16[16,128,128]{2,1,0:T(8,128)(2,1)S(1)}, u32[]{:S(2)}, u32[]{:S(2)}) %all-to-all-start) | async-done | bytes 524320 | tf_op jit(solution)/shard_map/all_to_all | solution.py:17
  25.2 5.8 %multiply_reduce_fusion = (f32[256,2048]{1,0:T(8,128)S(1)}, f32[256,4,2048]{2,0,1:T(8,128)}) fusion(f32[256,4]{0,1:T(4,128)} %param.12, bf16[2048,128,1]{1,0,2:T(8,128)(2,1)S(1)} %bitcast.31, bf16[256,4,128]{2,1,0:T(4,128)(2,1)} %param.10), kind=kOutput, calls=%fused_computation.6 | convolution fusion | flops 544735232 | bytes 11276288 | tf_op jit(solution)/shard_map/tjd,sd->tjs/dot_general | solution.py:60
  31.0 21.6 %all-gather.3.cloned.1.call-done = bf16[2048,576]{0,1:T(8,128)(2,1)} async-done(((bf16[128,576]{0,1:T(8,128)(2,1)}), bf16[2048,576]{0,1:T(8,128)(2,1)}) %all-gather.3.cloned.1.call-update) | async-done | bytes 2359312 | tf_op jit(solution)/shard_map/all_gather | solution.py:65
  52.6 13.1 %fusion.1 = f32[256,2048]{1,0:T(8,128)S(1)} fusion(bf16[2048,576]{0,1:T(8,128)(2,1)} %all-gather.3.cloned.1.call-done, f32[256,8]{1,0:T(8,128)S(1)} %copy.22, bf16[256,8,576]{2,1,0:T(8,128)(2,1)} %copy.21), kind=kOutput, calls=%fused_computation.2 | convolution fusion | flops 4843896832 | bytes 6823936 | tf_op jit(solution)/shard_map/rc,sc->rs/dot_general | solution.py:68
  65.7 1.3 broadcast_in_dim.42
  67.4 2.4 pad_maximum_fusion
  70.3 95.6 %reduce-scatter.2.cloned.1.call-done = f32[16,4096]{1,0:T(8,128)} async-done(((f32[256,4096]{1,0:T(8,128)}), f32[16,4096]{1,0:T(8,128)}) %reduce-scatter.2.cloned.1.call-update) | async-done | bytes 262160 | tf_op jit(solution)/shard_map/reduce_scatter | solution.py:27
  165.9 1.0 select_reduce_fusion
  167.0 1.2 fusion.24
  168.1 1.7 divide_subtract_fusion
  169.9 4.8 %fusion.16 = u8[256,2048]{1,0:T(8,128)(4,1)S(1)} fusion(f32[256,4,2048]{2,0,1:T(8,128)} %get-tuple-element.11), kind=kLoop, calls=%fused_computation.22 | loop fusion | flops 12058624 | bytes 8912896
  174.7 52.6 %all-gather.5.cloned.1.call-done = f32[256,2048]{1,0:T(8,128)} async-done(((f32[16,2048]{1,0:T(8,128)}), f32[256,2048]{1,0:T(8,128)}) %all-gather.5.cloned.1.call-update) | async-done | bytes 2097168 | tf_op jit(solution)/shard_map/all_gather | solution.py:76
  227.3 3.6 %fusion.15 = bf16[2048,128]{1,0:T(8,128)(2,1)S(1)} fusion(f32[256,2048]{1,0:T(8,128)} %all-gather.5.cloned.1.call-done, f32[256,4]{0,1:T(4,128)S(1)} %copy-done.1, u8[256,2048]{1,0:T(8,128)(4,1)S(1)} %fusion.16, bf16[256,4,128]{2,1,0:T(4,128)(2,1)S(1)} %copy-done), kind=kOutput, calls=%fused_computation.21 | convolution fusion | flops 552075264 | bytes 3411968 | tf_op jit(solution)/shard_map/tjs,tjd->sd/dot_general | solution.py:88
  231.0 15.3 %all_to_all.15 = bf16[16,128,128]{2,1,0:T(8,128)(2,1)S(1)} all-to-all(bf16[16,128,128]{2,1,0:T(8,128)(2,1)S(1)} %bitcast.36), channel_id=1, replica_groups=mesh['seq'=16,'head'=16] {'seq'}, dimensions={0} | all-to-all | bytes 1048576 | tf_op jit(solution)/shard_map/all_to_all | solution.py:38
  246.3 0.9 broadcast_in_dim.47
  247.2 6.2 %all-to-all-start.2 = ((bf16[16,128,128]{2,1,0:T(8,128)(2,1)}), bf16[16,128,128]{2,1,0:T(8,128)(2,1)S(1)}, u32[]{:S(2)}, u32[]{:S(2)}) async-start(bf16[16,128,128]{2,1,0:T(8,128)(2,1)} %broadcast_in_dim.47), calls=%async_computation.3 | async-start | bytes 1048576 | tf_op jit(solution)/shard_map/all_to_all | solution.py:17
  253.4 3.1 %fusion.18 = bf16[256,4,128]{2,0,1:T(8,128)(2,1)S(1)} fusion(bf16[2048,128,1]{1,0,2:T(8,128)(2,1)S(1)} %bitcast.32, f32[256,2048]{1,0:T(8,128)} %all-gather.5.cloned.1.call-done, f32[256,4]{0,1:T(4,128)S(1)} %copy-done.1, u8[256,2048]{1,0:T(8,128)(4,1)S(1)} %fusion.16), kind=kOutput, calls=%fused_computation.25 | convolution fusion | flops 551813120 | bytes 3411968 | tf_op jit(solution)/shard_map/tjs,sd->tjd/dot_general | solution.py:83
  256.6 0.9 copy.25
  257.5 14.3 %all-to-all-done.2 = bf16[16,128,128]{2,1,0:T(8,128)(2,1)S(1)} async-done(((bf16[16,128,128]{2,1,0:T(8,128)(2,1)}), bf16[16,128,128]{2,1,0:T(8,128)(2,1)S(1)}, u32[]{:S(2)}, u32[]{:S(2)}) %all-to-all-start.2) | async-done | bytes 524320 | tf_op jit(solution)/shard_map/all_to_all | solution.py:17
  271.8 0.7 convert_reduce_fusion
  (15 shorter events, 2.5 us)
Async XLA Ops:
  7.2 45.5 %all-gather.3.cloned.1.call-start = ((), (), s32[]{:S(2)}) async-start(), calls=%async_computation.4 | async-start | bytes 2506752 | tf_op jit(solution)/shard_map/all_gather | solution.py:65
  9.5 15.6 %all-to-all-start = ((bf16[16,128,128]{2,1,0:T(8,128)(2,1)}), bf16[16,128,128]{2,1,0:T(8,128)(2,1)S(1)}, u32[]{:S(2)}, u32[]{:S(2)}) async-start(bf16[16,128,128]{2,1,0:T(8,128)(2,1)} %broadcast_in_dim.40), calls=%async_computation | async-start | bytes 1048576 | tf_op jit(solution)/shard_map/all_to_all | solution.py:17
  15.5 150.4 %reduce-scatter.2.cloned.1.call-start = ((), (), s32[]{:S(2)}) async-start(), calls=%async_computation.5 | async-start | bytes 4456448 | tf_op jit(solution)/shard_map/reduce_scatter | solution.py:27
  69.7 157.6 %copy-start = (bf16[256,4,128]{2,1,0:T(4,128)(2,1)S(1)}, bf16[256,4,128]{2,1,0:T(4,128)(2,1)}, u32[]{:S(2)}) copy-start(bf16[256,4,128]{2,1,0:T(4,128)(2,1)} %param.10) | copy-start | bytes 786436
  69.7 157.6 %copy-start.1 = (f32[256,4]{0,1:T(4,128)S(1)}, f32[256,4]{0,1:T(4,128)}, u32[]{:S(2)}) copy-start(f32[256,4]{0,1:T(4,128)} %param.12) | copy-start | bytes 12292
  69.8 157.5 %all-gather.5.cloned.1.call-start = ((), (), s32[]{:S(2)}) async-start(), calls=%async_computation.6 | async-start | bytes 2228224 | tf_op jit(solution)/shard_map/all_gather | solution.py:76
  247.2 24.6 %all-to-all-start.2 = ((bf16[16,128,128]{2,1,0:T(8,128)(2,1)}), bf16[16,128,128]{2,1,0:T(8,128)(2,1)S(1)}, u32[]{:S(2)}, u32[]{:S(2)}) async-start(bf16[16,128,128]{2,1,0:T(8,128)(2,1)} %broadcast_in_dim.47), calls=%async_computation.3 | async-start | bytes 1048576 | tf_op jit(solution)/shard_map/all_to_all | solution.py:17
Sparse Core Ops, SparseCore 0:
  9.7 42.8 all-gather.2
  69.9 95.9 reduce-scatter.1
  170.0 57.2 all-gather.4
where the time goes:
time: 280 us; the launch traced here: 279 us
  waiting for transfers between devices  188 us (67%)
  matrix products  25.7 us (9%)
  blocking collectives  15.3 us (5%)
  between operations  13.8 us (5%)
  other arithmetic  13 us (5%)
  starting transfers between devices  12.5 us (4%)
  local copies, waits for them, and re-layouts  10.8 us (4%)
    reduce_scatter x1, waiting for transfers between devices, sent_together(): out = lax.psum_scatter(both, axis, scatter_dimension=dim, tiled=True)  95.6 us
    all_gather x1, waiting for transfers between devices, local(): lax.all_gather(logit_gradient(head_sum, logit, keep_share), 'head', axis=...  52.6 us
    all_gather x1, waiting for transfers between devices, local(): piece = lax.all_gather(key_latent, 'seq', axis=0, tiled=True)  21.6 us
    all_to_all x2, waiting for transfers between devices, from_everyone(): return lax.all_to_all(copies, axis, split_axis=0, concat_axis=0, tiled=True)  17.5 us
    all_to_all x1, blocking collectives, sent_and_summed(): tiles = lax.all_to_all(cut_along(value, dim, count), axis, 0, 0, tiled=True)  15.3 us
    dot_general x1, matrix products, local(): jnp.einsum('rc,sc->rs', flat_query, piece, preferred_element_type=jnp.flo...  13.1 us
    all_to_all x2, starting transfers between devices, from_everyone(): return lax.all_to_all(copies, axis, split_axis=0, concat_axis=0, tiled=True)  12.2 us
    unnamed x8, local copies, waits for them, and re-layouts  6.97 us
  transfers between devices with their start and end apart: 5, of which 5 were waited for; matrix products, arithmetic and copies ran while one was open for 8% of the time, Pallas kernels for 0%

commit v1 on v0

--- a/solution.py
+++ b/solution.py
@@ -62,7 +62,10 @@
     )
     logit_part = jnp.sum(index_weight[:, :, None] * jnp.maximum(z_val, 0.0), axis=1)
     flat_query = query_latent.reshape(query_rows * head_count, width)
-    piece = lax.all_gather(key_latent, "seq", axis=0, tiled=True)
+    peers = lax.axis_size("seq")
+    parts = jnp.stack([key_latent for _ in range(peers)])
+    parts = lax.all_to_all(parts, "seq", split_axis=0, concat_axis=0)
+    piece = jnp.concatenate(parts, axis=0)
     count = piece.shape[0]
     scores = (
         jnp.einsum("rc,sc->rs", flat_query, piece, preferred_element_type=jnp.float32) * attn_scale

time: 280 us -> 290 us (1.036)
  blocking collectives: 15.3 us -> 30.8 us
  waiting for transfers between devices: 188 us -> 185 us
    all_gather x1 -> x0, waiting for transfers between devices: 21.6 us -> none  [local(): piece = lax.all_gather(key_latent, 'seq', axis=0, tiled=True)]
    all_to_all x0 -> x1, waiting for transfers between devices: none -> 20.9 us  [local(): parts = lax.all_to_all(parts, 'seq', split_axis=0, concat_axis=0)]
    all_to_all x0 -> x1, blocking collectives: none -> 15.6 us  [from_everyone(): return lax.all_to_all(copies, axis, split_axis=0, concat_axis=0, tiled=True)]
    all_to_all x2 -> x1, starting transfers between devices: 12.2 us -> 6.23 us  [from_everyone(): return lax.all_to_all(copies, axis, split_axis=0, concat_axis=0, tiled=True)]
    all_to_all x0 -> x1, starting transfers between devices: none -> 5.55 us  [local(): parts = lax.all_to_all(parts, 'seq', split_axis=0, concat_axis=0)]
    all_to_all x2 -> x1, waiting for transfers between devices: 17.5 us -> 14.3 us  [from_everyone(): return lax.all_to_all(copies, axis, split_axis=0, concat_axis=0, tiled=True)]
    unnamed x8 -> x14, local copies, waits for them, and re-layouts: 6.97 us -> 4.87 us
  transfers between devices with their start and end apart: 5 -> 4, of which waited for: 5 -> 4; matrix products, arithmetic and copies ran while one was open for 8% -> 6% of each run, Pallas kernels for 0% -> 0%
where the time goes in v1:
time: 290 us; the launch traced here: 289 us
  waiting for transfers between devices  185 us (64%)
  blocking collectives  30.8 us (11%)
  matrix products  24.4 us (8%)
  between operations  14.2 us (5%)
  other arithmetic  12.3 us (4%)
  starting transfers between devices  12 us (4%)
  local copies, waits for them, and re-layouts  10.6 us (4%)
    reduce_scatter x1, waiting for transfers between devices, sent_together(): out = lax.psum_scatter(both, axis, scatter_dimension=dim, tiled=True)  96.8 us
    all_gather x1, waiting for transfers between devices, local(): lax.all_gather(logit_gradient(head_sum, logit, keep_share), 'head', axis=...  52.6 us
    all_to_all x1, waiting for transfers between devices, local(): parts = lax.all_to_all(parts, 'seq', split_axis=0, concat_axis=0)  20.9 us
    all_to_all x1, blocking collectives, from_everyone(): return lax.all_to_all(copies, axis, split_axis=0, concat_axis=0, tiled=True)  15.6 us
    all_to_all x1, blocking collectives, sent_and_summed(): tiles = lax.all_to_all(cut_along(value, dim, count), axis, 0, 0, tiled=True)  15.3 us
    all_to_all x1, waiting for transfers between devices, from_everyone(): return lax.all_to_all(copies, axis, split_axis=0, concat_axis=0, tiled=True)  14.3 us
    dot_general x1, matrix products, local(): jnp.einsum('rc,sc->rs', flat_query, piece, preferred_element_type=jnp.flo...  12.7 us
    all_to_all x1, starting transfers between devices, from_everyone(): return lax.all_to_all(copies, axis, split_axis=0, concat_axis=0, tiled=True)  6.23 us
  transfers between devices with their start and end apart: 4, of which 4 were waited for; matrix products, arithmetic and copies ran while one was open for 6% of the time, Pallas kernels for 0%

profile of v1, /device:TPU:32, one launch (start us, length us, event | category | flops | bytes accessed | tf_op | source)
XLA Modules:
  0.0 289.1 jit_solution(5512112382199118184)
XLA Ops:
  7.2 0.9 broadcast_in_dim.40
  8.0 15.6 %all_to_all.20 = bf16[16,128,128]{2,1,0:T(8,128)(2,1)S(1)} all-to-all(bf16[16,128,128]{2,1,0:T(8,128)(2,1)S(1)} %broadcast_in_dim.40), channel_id=1, replica_groups=mesh['seq'=16,'head'=16] {'seq'}, dimensions={0} | all-to-all | bytes 1048576 | tf_op jit(solution)/shard_map/all_to_all | solution.py:17
  23.6 2.7 stack.2
  26.4 5.5 %all-to-all-start.1 = ((bf16[16,128,576]{1,2,0:T(8,128)(2,1)}), bf16[16,128,576]{1,2,0:T(8,128)(2,1)}, u32[]{:S(2)}, u32[]{:S(2)}) async-start(bf16[16,128,576]{1,2,0:T(8,128)(2,1)} %stack.2), calls=%async_computation.1 | async-start | bytes 4718592 | tf_op jit(solution)/shard_map/all_to_all | solution.py:67
  32.1 3.5 %copy.36 = bf16[256,8,576]{2,1,0:T(8,128)(2,1)} copy(bf16[256,8,576]{0,2,1:T(8,128)(2,1)S(1)} %copy-done) | data formatting | bytes 4718592 | tf_op args[0]
  35.6 4.9 %multiply_reduce_fusion = (f32[256,2048]{1,0:T(8,128)S(1)}, f32[256,4,2048]{2,0,1:T(8,128)}) fusion(f32[256,4]{0,1:T(4,128)S(1)} %copy-done.3, bf16[2048,128,1]{1,0,2:T(8,128)(2,1)S(1)} %bitcast.37, bf16[256,4,128]{2,1,0:T(4,128)(2,1)S(1)} %copy-done.1), kind=kOutput, calls=%fused_computation.6 | convolution fusion | flops 544735232 | bytes 11276288 | tf_op jit(solution)/shard_map/tjd,sd->tjs/dot_general | solution.py:60
  40.5 20.9 %all-to-all-done.1 = bf16[16,128,576]{1,2,0:T(8,128)(2,1)} async-done(((bf16[16,128,576]{1,2,0:T(8,128)(2,1)}), bf16[16,128,576]{1,2,0:T(8,128)(2,1)}, u32[]{:S(2)}, u32[]{:S(2)}) %all-to-all-start.1) | async-done | bytes 2359328 | tf_op jit(solution)/shard_map/all_to_all | solution.py:67
  61.5 12.7 %fusion.1 = f32[256,2048]{1,0:T(8,128)S(1)} fusion(f32[256,8]{1,0:T(8,128)S(1)} %copy.38, bf16[256,8,576]{2,1,0:T(8,128)(2,1)} %copy.36, bf16[16,128,576]{1,2,0:T(8,128)(2,1)} %all-to-all-done.1), kind=kOutput, calls=%fused_computation.2 | convolution fusion | flops 4843896832 | bytes 6823936 | tf_op jit(solution)/shard_map/rc,sc->rs/dot_general | solution.py:71
  74.2 1.3 broadcast_in_dim.42
  75.9 2.4 pad_maximum_fusion
  78.8 96.8 %reduce-scatter.2.cloned.1.call-done = f32[16,4096]{1,0:T(8,128)} async-done(((f32[256,4096]{1,0:T(8,128)}), f32[16,4096]{1,0:T(8,128)}) %reduce-scatter.2.cloned.1.call-update) | async-done | bytes 262160 | tf_op jit(solution)/shard_map/reduce_scatter | solution.py:27
  175.6 1.0 select_reduce_fusion
  176.7 1.2 fusion.26
  177.9 1.7 divide_subtract_fusion
  179.6 4.8 %fusion.18 = u8[256,2048]{1,0:T(8,128)(4,1)S(1)} fusion(f32[256,4,2048]{2,0,1:T(8,128)} %get-tuple-element.15), kind=kLoop, calls=%fused_computation.24 | loop fusion | flops 12058624 | bytes 8912896
  184.4 52.6 %all-gather.2.cloned.1.call-done = f32[256,2048]{1,0:T(8,128)} async-done(((f32[16,2048]{1,0:T(8,128)}), f32[256,2048]{1,0:T(8,128)}) %all-gather.2.cloned.1.call-update) | async-done | bytes 2097168 | tf_op jit(solution)/shard_map/all_gather | solution.py:79
  237.0 3.6 %fusion.15 = bf16[2048,128]{1,0:T(8,128)(2,1)S(1)} fusion(f32[256,2048]{1,0:T(8,128)} %all-gather.2.cloned.1.call-done, f32[256,4]{0,1:T(4,128)S(1)} %copy-done.3, u8[256,2048]{1,0:T(8,128)(4,1)S(1)} %fusion.18, bf16[256,4,128]{2,1,0:T(4,128)(2,1)S(1)} %copy-done.1), kind=kOutput, calls=%fused_computation.21 | convolution fusion | flops 552075264 | bytes 3411968 | tf_op jit(solution)/shard_map/tjs,tjd->sd/dot_general | solution.py:91
  240.7 15.3 %all_to_all.21 = bf16[16,128,128]{2,1,0:T(8,128)(2,1)S(1)} all-to-all(bf16[16,128,128]{2,1,0:T(8,128)(2,1)S(1)} %bitcast.42), channel_id=1, replica_groups=mesh['seq'=16,'head'=16] {'seq'}, dimensions={0} | all-to-all | bytes 1048576 | tf_op jit(solution)/shard_map/all_to_all | solution.py:38
  256.0 0.9 broadcast_in_dim.47
  256.9 6.2 %all-to-all-start.3 = ((bf16[16,128,128]{2,1,0:T(8,128)(2,1)}), bf16[16,128,128]{2,1,0:T(8,128)(2,1)S(1)}, u32[]{:S(2)}, u32[]{:S(2)}) async-start(bf16[16,128,128]{2,1,0:T(8,128)(2,1)} %broadcast_in_dim.47), calls=%async_computation.4 | async-start | bytes 1048576 | tf_op jit(solution)/shard_map/all_to_all | solution.py:17
  263.2 3.1 %fusion.20 = bf16[256,4,128]{2,0,1:T(8,128)(2,1)S(1)} fusion(bf16[2048,128,1]{1,0,2:T(8,128)(2,1)S(1)} %bitcast.38, f32[256,2048]{1,0:T(8,128)} %all-gather.2.cloned.1.call-done, f32[256,4]{0,1:T(4,128)S(1)} %copy-done.3, u8[256,2048]{1,0:T(8,128)(4,1)S(1)} %fusion.18), kind=kOutput, calls=%fused_computation.27 | convolution fusion | flops 551813120 | bytes 3411968 | tf_op jit(solution)/shard_map/tjs,sd->tjd/dot_general | solution.py:86
  266.3 0.9 copy.41
  267.2 14.3 %all-to-all-done.3 = bf16[16,128,128]{2,1,0:T(8,128)(2,1)S(1)} async-done(((bf16[16,128,128]{2,1,0:T(8,128)(2,1)}), bf16[16,128,128]{2,1,0:T(8,128)(2,1)S(1)}, u32[]{:S(2)}, u32[]{:S(2)}) %all-to-all-start.3) | async-done | bytes 524320 | tf_op jit(solution)/shard_map/all_to_all | solution.py:17
  281.5 0.7 convert_reduce_fusion
  (20 shorter events, 1.2 us)
Async XLA Ops:
  8.0 23.9 %copy-start.2 = (f32[256,8]{0,1:T(8,128)S(1)}, f32[256,8]{0,1:T(8,128)}, u32[]{:S(2)}) copy-start(f32[256,8]{0,1:T(8,128)} %param.9) | copy-start | bytes 24580
  8.0 24.1 %copy-start = (bf16[256,8,576]{0,2,1:T(8,128)(2,1)S(1)}, bf16[256,8,576]{0,2,1:T(8,128)(2,1)}, u32[]{:S(2)}) copy-start(bf16[256,8,576]{0,2,1:T(8,128)(2,1)} %param.7) | copy-start | bytes 7077892
  26.4 9.3 %copy-start.4 = (s32[2,16]{1,0:T(2,128)S(1)}, s32[2,16]{1,0:T(2,128)}, u32[]{:S(2)}) copy-start(s32[2,16]{1,0:T(2,128)} %param.13) | copy-start | bytes 388
  26.4 9.3 %copy-start.1 = (bf16[256,4,128]{2,1,0:T(4,128)(2,1)S(1)}, bf16[256,4,128]{2,1,0:T(4,128)(2,1)}, u32[]{:S(2)}) copy-start(bf16[256,4,128]{2,1,0:T(4,128)(2,1)} %param.10) | copy-start | bytes 786436
  26.4 9.3 %copy-start.3 = (f32[256,4]{0,1:T(4,128)S(1)}, f32[256,4]{0,1:T(4,128)}, u32[]{:S(2)}) copy-start(f32[256,4]{0,1:T(4,128)} %param.12) | copy-start | bytes 12292
  26.4 35.1 %all-to-all-start.1 = ((bf16[16,128,576]{1,2,0:T(8,128)(2,1)}), bf16[16,128,576]{1,2,0:T(8,128)(2,1)}, u32[]{:S(2)}, u32[]{:S(2)}) async-start(bf16[16,128,576]{1,2,0:T(8,128)(2,1)} %stack.2), calls=%async_computation.1 | async-start | bytes 4718592 | tf_op jit(solution)/shard_map/all_to_all | solution.py:67
  31.9 143.7 %reduce-scatter.2.cloned.1.call-start = ((), (), s32[]{:S(2)}) async-start(), calls=%async_computation.5 | async-start | bytes 4456448 | tf_op jit(solution)/shard_map/reduce_scatter | solution.py:27
  78.3 158.8 %all-gather.2.cloned.1.call-start = ((), (), s32[]{:S(2)}) async-start(), calls=%async_computation.6 | async-start | bytes 2228224 | tf_op jit(solution)/shard_map/all_gather | solution.py:79
  256.9 24.6 %all-to-all-start.3 = ((bf16[16,128,128]{2,1,0:T(8,128)(2,1)}), bf16[16,128,128]{2,1,0:T(8,128)(2,1)S(1)}, u32[]{:S(2)}, u32[]{:S(2)}) async-start(bf16[16,128,128]{2,1,0:T(8,128)(2,1)} %broadcast_in_dim.47), calls=%async_computation.4 | async-start | bytes 1048576 | tf_op jit(solution)/shard_map/all_to_all | solution.py:17
Sparse Core Ops, SparseCore 0:
  78.4 97.1 reduce-scatter.1
  179.7 57.2 all-gather.1
